TPU v7x, 128 devices: a whole 4x4x4 slice. The times are simulated.
128 devices in a mesh: axial: 4 (over x), azim: 32 (over z, y, core).
Axes of the slice: x: 4, y: 4, z: 4, core: 2. Of those that a mesh axis runs over, the one named last changes fastest.
Arguments:
- density: float32 [64, 256, 512], P(None, 'azim', 'axial'), may hold values from 0.5 to 2
- velocity: float32 [3, 64, 256, 512], P(None, None, 'azim', 'axial'), may hold values from -3 to 3
- pressure: float32 [64, 256, 512], P(None, 'azim', 'axial'), may hold values from 0.4 to 1.5
- axial_metric: float32 [3, 64, 256, 512], P(None, None, 'azim', 'axial'), may hold values from -4 to 4
- azim_metric: float32 [3, 64, 256, 512], P(None, None, 'azim', 'axial'), may hold values from -4 to 4
- volume: float32 [64, 256, 512], P(None, 'azim', 'axial'), may hold values from 0.5 to 2
- radial_term: float32 [5, 64, 256, 512], P(None, None, 'azim', 'axial'), may hold values from -6 to 6
- panel_area: float32 [256, 512], P('azim', 'axial'), may hold values from 0.5 to 2
- observer_ids: int32 [4, 256, 512], P(None, 'azim', 'axial'), may hold values from 0 to 511
- bin_ids: int32 [4, 256, 512], P(None, 'azim', 'axial'), may hold values from 0 to 127
- weight_ids: int32 [4, 256, 512], P(None, 'azim', 'axial'), may hold values from 0 to 255
- bin_weights: float32 [256], replicated, may hold values from 0.2 to 1
Outputs:
- new_state: float32 [5, 64, 256, 512], P(None, None, 'azim', 'axial')
- signals: float32 [512, 128], P(('axial', 'azim'))
All inputs are finite; a program needn't handle non-finite values.
Results may differ from a plain program's by a relative error of at most 0.0003.
Values sent between devices are 32-bit elements; how exact they have to be, the bound alone decides.
A program may use at most 128 MiB of HBM per device.

v0:
```python
import math
import jax
import jax.numpy as jnp
from jax import lax
from jax.sharding import PartitionSpec as P

OBSERVERS = 512
TIME_BINS = 128
GAMMA = 1.4
SECTION = 0.25
DERIV_ALPHA = 1.0 / 3.0
FILTER_ALPHA = 0.499
DERIV_A = 14.0 / 9.0
DERIV_B = 1.0 / 9.0
HIGHEST = lax.Precision.HIGHEST


def padded(cells, sides, width, closed):
    for axis, dim in sides:
        count = lax.axis_size(axis)
        ends = count if closed else count - 1
        head = lax.slice_in_dim(cells, 0, width, axis=dim)
        tail = lax.slice_in_dim(cells, cells.shape[dim] - width, cells.shape[dim], axis=dim)
        cells = jnp.concatenate(
            [
                lax.ppermute(tail, axis, [(i, (i + 1) % count) for i in range(ends)]),
                cells,
                lax.ppermute(head, axis, [((i + 1) % count, i) for i in range(ends)]),
            ],
            axis=dim,
        )
    return cells


def decay_root(alpha):
    return (-1.0 + math.sqrt(1.0 - 4.0 * alpha * alpha)) / (2.0 * alpha)


def signed_power(base, exponent):
    exponent = jnp.asarray(exponent)
    parity = jnp.where(exponent % 2 == 0, 1.0, -1.0)
    return parity * jnp.exp(exponent.astype(jnp.float32) * math.log(-base))


def deriv_side(extended, dim):
    length = extended.shape[dim] - 6

    def cells(offset):
        return lax.slice_in_dim(extended, 3 + offset, 3 + offset + length, axis=dim)

    return 0.5 * DERIV_A * (cells(1) - cells(-1)) + 0.25 * DERIV_B * (cells(2) - cells(-2))


def filter_side(extended, dim):
    length = extended.shape[dim] - 6

    def cells(offset):
        return lax.slice_in_dim(extended, 3 + offset, 3 + offset + length, axis=dim)

    beta = FILTER_ALPHA
    coeffs = [
        (11.0 + 10.0 * beta) / 16.0,
        (15.0 + 34.0 * beta) / 32.0,
        (-3.0 + 6.0 * beta) / 16.0,
        (1.0 - 2.0 * beta) / 32.0,
    ]
    total = coeffs[0] * cells(0)
    for shift in range(1, 4):
        total = total + 0.5 * coeffs[shift] * (cells(shift) + cells(-shift))
    return total


def fluxes(density, velocity, pressure, energy, metric, volume):
    contra = metric[0] * velocity[0] + metric[1] * velocity[1] + metric[2] * velocity[2]
    mass_flow = density * contra
    pieces = [volume * mass_flow]
    for comp in range(3):
        pieces.append(volume * (mass_flow * velocity[comp] + metric[comp] * pressure))
    pieces.append(volume * (energy + pressure) * contra)
    return jnp.stack(pieces)


def pad_axial(field):
    return padded(field, (("axial", 3),), 3, False)


def pad_azimuth(field):
    return padded(field, (("azim", 2),), 3, True)


def open_line(rhs, alpha):
    base = decay_root(alpha)
    factor_g = -alpha / base
    scale = 1.0 / (factor_g * (1.0 - base * base))
    width_here = rhs.shape[3]
    group_size = lax.axis_size("axial")
    device_pos = lax.axis_index("axial")
    total_len = width_here * group_size
    offsets = jnp.arange(width_here, dtype=jnp.int32)
    local_matrix = signed_power(base, jnp.abs(offsets[:, None] - offsets[None, :]))
    local_part = jnp.einsum("vraj,ij->vrai", rhs, local_matrix, precision=HIGHEST)
    first_moment = jnp.einsum(
        "vraj,j->vra", rhs, signed_power(base, width_here - 1 - offsets), precision=HIGHEST
    )
    last_moment = jnp.einsum("vraj,j->vra", rhs, signed_power(base, offsets), precision=HIGHEST)
    moments = jnp.stack([first_moment, last_moment])[None]
    piece = lax.all_gather(moments, "axial", axis=0, tiled=True)
    others = jnp.arange(piece.shape[0], dtype=jnp.int32)
    gap_up = device_pos - others
    w_left = jnp.where(
        gap_up > 0, signed_power(base, width_here * jnp.maximum(gap_up - 1, 0) + 1), 0.0
    )
    w_right = jnp.where(
        gap_up < 0, signed_power(base, width_here * jnp.maximum(-gap_up - 1, 0) + 1), 0.0
    )
    w_end = signed_power(base, width_here * (group_size - 1 - others))
    left_sum = jnp.einsum("k,kvra->vra", w_left, piece[:, 0], precision=HIGHEST)
    right_sum = jnp.einsum("k,kvra->vra", w_right, piece[:, 1], precision=HIGHEST)
    end_sum = jnp.einsum("k,kvra->vra", w_end, piece[:, 0], precision=HIGHEST)
    left_sum, right_sum, end_sum = (left_sum, right_sum, end_sum)
    position = device_pos * width_here + offsets
    result = local_part + signed_power(base, offsets) * left_sum[..., None]
    result = result + signed_power(base, width_here - 1 - offsets) * right_sum[..., None]
    result = result - signed_power(base, total_len + 1 - position) * end_sum[..., None]
    return scale * result


def cycle_line(rhs, alpha):
    base = decay_root(alpha)
    factor_g = -alpha / base
    width_here = rhs.shape[2]
    group_size = lax.axis_size("azim")
    device_pos = lax.axis_index("azim")
    total_len = width_here * group_size
    scale = 1.0 / (factor_g * (1.0 - base * base) * (1.0 - base**total_len))
    offsets = jnp.arange(width_here, dtype=jnp.int32)
    gap = jnp.abs(offsets[:, None] - offsets[None, :])
    local_matrix = scale * (signed_power(base, gap) + signed_power(base, total_len - gap))
    local_part = jnp.einsum("vrjx,ij->vrix", rhs, local_matrix, precision=HIGHEST)
    first_moment = jnp.einsum(
        "vrjx,j->vrx", rhs, signed_power(base, width_here - 1 - offsets), precision=HIGHEST
    )
    last_moment = jnp.einsum("vrjx,j->vrx", rhs, signed_power(base, offsets), precision=HIGHEST)
    moments = jnp.stack([first_moment, last_moment])[None]
    piece = lax.all_gather(moments, "azim", axis=0, tiled=True)
    others = jnp.arange(piece.shape[0], dtype=jnp.int32)
    shift = (device_pos - others) % group_size
    w_first = jnp.where(
        shift > 0, signed_power(base, width_here * jnp.maximum(shift - 1, 0) + 1), 0.0
    )
    w_last = jnp.where(
        shift > 0, signed_power(base, width_here * jnp.maximum(group_size - shift - 1, 0) + 1), 0.0
    )
    first_sum = jnp.einsum("k,kvrx->vrx", w_first, piece[:, 0], precision=HIGHEST)
    last_sum = jnp.einsum("k,kvrx->vrx", w_last, piece[:, 1], precision=HIGHEST)
    outer = signed_power(base, offsets)[:, None] * first_sum[:, :, None, :]
    outer = outer + signed_power(base, width_here - 1 - offsets)[:, None] * last_sum[:, :, None, :]
    return local_part + scale * outer


def per_device(
    density,
    velocity,
    pressure,
    axial_metric,
    azim_metric,
    volume,
    radial_term,
    panel_area,
    observer_ids,
    bin_ids,
    weight_ids,
    bin_weights,
):
    energy = pressure / (GAMMA - 1.0) + 0.5 * density * (
        velocity[0] ** 2 + velocity[1] ** 2 + velocity[2] ** 2
    )
    state = jnp.concatenate([density[None], density[None] * velocity, energy[None]], axis=0)
    axial_flux = fluxes(density, velocity, pressure, energy, axial_metric, volume)
    azim_flux = fluxes(density, velocity, pressure, energy, azim_metric, volume)
    axial_deriv = open_line(deriv_side(pad_axial(axial_flux), 3), DERIV_ALPHA)
    azim_deriv = cycle_line(deriv_side(pad_azimuth(azim_flux), 2), DERIV_ALPHA)
    sectioned = state + SECTION * (radial_term - (axial_deriv + azim_deriv) / volume)
    smoothed = open_line(filter_side(pad_axial(sectioned), 3), FILTER_ALPHA)
    new_state = cycle_line(filter_side(pad_azimuth(smoothed), 2), FILTER_ALPHA)
    surface = new_state[:, 0]
    source = panel_area * (surface[2] + surface[0] - 1.0)
    table_size = bin_weights.shape[0]
    one_hot = (
        weight_ids.reshape(-1)[:, None] == jnp.arange(table_size, dtype=jnp.int32)[None, :]
    ).astype(jnp.float32)
    entry_weight = jnp.dot(one_hot, bin_weights, precision=HIGHEST)
    values = entry_weight * jnp.broadcast_to(source[None], weight_ids.shape).reshape(-1)
    bucket = (observer_ids * TIME_BINS + bin_ids).reshape(-1)
    partial_signals = jax.ops.segment_sum(
        values, bucket, num_segments=OBSERVERS * TIME_BINS
    ).reshape(OBSERVERS, TIME_BINS)
    signals = lax.psum_scatter(partial_signals, ("axial", "azim"), scatter_dimension=0, tiled=True)
    return (new_state, signals)


def solution(mesh):
    placed = (
        P(None, "azim", "axial"),
        P(None, None, "azim", "axial"),
        P(None, "azim", "axial"),
        P(None, None, "azim", "axial"),
        P(None, None, "azim", "axial"),
        P(None, "azim", "axial"),
        P(None, None, "azim", "axial"),
        P("azim", "axial"),
        P(None, "azim", "axial"),
        P(None, "azim", "axial"),
        P(None, "azim", "axial"),
        P(),
    )
    return jax.shard_map(
        per_device,
        mesh=mesh,
        in_specs=placed,
        out_specs=(P(None, None, "azim", "axial"), P(("axial", "azim"), None)),
        check_vma=False,
    )
```

profile of v0, /device:TPU:1, one launch (start us, length us, event | category | flops | bytes accessed | tf_op | source)
XLA Modules:
  0.0 457.5 jit_solution(16983114548345051890)
XLA Ops:
  7.3 2.7 bitcast_dynamic-update-slice_fusion.4
  15.6 6.4 %collective-permute-done.2 = f32[5,64,3,128]{3,1,2,0:T(8,128)S(1)} collective-permute-done((f32[5,64,3,128]{3,1,2,0:T(8,128)S(1)}, f32[5,64,3,128]{3,1,2,0:T(8,128)S(1)}, u32[]{:S(2)}, u32[]{:S(2)}) %collective-permute-start.2) | collective-permute-done | bytes 491552 | tf_op jit(solution)/shard_map/ppermute | solution.py:28
  28.7 1.8 copy.14
  32.8 4.2 collective-permute-start.1
  37.6 1.9 broadcast_multiply_fusion.1
  39.5 1.6 copy.15
  42.7 5.7 %fusion.30 = f32[5,64,8,128]{3,2,1,0:T(8,128)S(1)} fusion(f32[5,64,8,3]{3,2,1,0:T(8,128)} %copy.17, f32[5,64,8,128]{3,2,1,0:T(8,128)S(1)} %bitcast_dynamic-update-slice_fusion.5, f32[5,64,8,3]{3,2,1,0:T(8,128)} %copy.15), kind=kLoop, calls=%fused_computation.64 | loop fusion | flops 2949120 | bytes 2682880 | tf_op jit(solution)/shard_map/add | solution.py:51
  48.3 17.3 %fusion.215 = f32[1,5,64,8]{3,0,2,1:T(1,128)S(1)} fusion(f32[5,64,8,128]{3,2,1,0:T(8,128)S(1)} %fusion.30), kind=kOutput, calls=%fused_computation.350 | convolution fusion | flops 3934336 | bytes 1320960 | tf_op jit(solution)/shard_map/vraj,j->vra/dot_general | solution.py:102
  65.7 17.7 %fusion.213 = f32[1,5,64,8]{3,0,2,1:T(1,128)S(1)} fusion(f32[5,64,8,128]{3,2,1,0:T(8,128)S(1)} %fusion.30), kind=kOutput, calls=%fused_computation.348 | convolution fusion | flops 3933568 | bytes 1320960 | tf_op jit(solution)/shard_map/vraj,j->vra/dot_general | solution.py:105
  83.5 9.9 %all-gather = f32[8,5,64,8]{2,3,1,0:T(8,128)S(1)} all-gather(f32[2,5,64,8]{2,3,1,0:T(8,128)S(1)} %pad_maximum_fusion.10), channel_id=2, replica_groups=mesh['axial'=4,'azim'=32] {'axial'}, dimensions={0}, use_global_device_ids=true | all-gather | bytes 102400 | tf_op jit(solution)/shard_map/all_gather | solution.py:107
  94.7 2.5 fusion.19
  97.3 5.2 %slice_bitcast_fusion.3 = (f32[32,5,64,128]{3,2,1,0:T(8,128)S(1)}, f32[32,5,64,128]{3,2,1,0:T(8,128)S(1)}) fusion(f32[32,2,5,64,128]{4,3,2,1,0:T(8,128)} %bitcast.355), kind=kLoop, calls=%fused_computation.4 | loop fusion | bytes 20971520 | tf_op jit(solution)/shard_map/squeeze | solution.py:154
  102.5 5.4 %fusion.6 = f32[1,5,64,128]{3,0,2,1:T(1,128)S(1)} fusion(f32[32,5,64,128]{3,2,1,0:T(8,128)S(1)} %get-tuple-element.12, s32[]{:T(128)S(6)} %axis_index.33), kind=kOutput, calls=%fused_computation.11 | convolution fusion | flops 15729728 | bytes 5406724 | tf_op jit(solution)/shard_map/k,kvrx->vrx/dot_general | solution.py:154
  108.0 5.6 %fusion.4 = f32[1,5,64,128]{3,0,2,1:T(1,128)S(1)} fusion(f32[32,5,64,128]{3,2,1,0:T(8,128)S(1)} %get-tuple-element.13, s32[]{:T(128)S(6)} %axis_index.33), kind=kOutput, calls=%fused_computation.9 | convolution fusion | flops 15729728 | bytes 5406724 | tf_op jit(solution)/shard_map/k,kvrx->vrx/dot_general | solution.py:155
  113.7 1.8 fusion.21
  117.0 1.8 copy.22
  120.5 4.0 collective-permute-start.5
  127.7 6.2 %fusion.47 = f32[5,64,8,128]{3,2,1,0:T(8,128)S(1)} fusion(f32[5,64,8,3]{3,2,1,0:T(8,128)} %copy.25, f32[5,64,8,128]{3,2,1,0:T(8,128)S(1)} %fusion.21, f32[5,64,8,3]{3,2,1,0:T(8,128)} %copy.23), kind=kLoop, calls=%fused_computation.81 | loop fusion | flops 5242880 | bytes 2682880 | tf_op jit(solution)/shard_map/add | solution.py:69
  133.8 17.3 %fusion.204 = f32[1,5,64,8]{3,0,2,1:T(1,128)S(1)} fusion(f32[5,64,8,128]{3,2,1,0:T(8,128)S(1)} %fusion.47), kind=kOutput, calls=%fused_computation.339 | convolution fusion | flops 3934336 | bytes 1320960 | tf_op jit(solution)/shard_map/vraj,j->vra/dot_general | solution.py:102
  151.1 17.7 %fusion.202 = f32[1,5,64,8]{3,0,2,1:T(1,128)S(1)} fusion(f32[5,64,8,128]{3,2,1,0:T(8,128)S(1)} %fusion.47), kind=kOutput, calls=%fused_computation.337 | convolution fusion | flops 3933568 | bytes 1320960 | tf_op jit(solution)/shard_map/vraj,j->vra/dot_general | solution.py:105
  169.0 9.2 %all-gather.2 = f32[8,5,64,8]{2,3,1,0:T(8,128)S(1)} all-gather(f32[2,5,64,8]{2,3,1,0:T(8,128)S(1)} %pad_maximum_fusion.11), channel_id=4, replica_groups=mesh['axial'=4,'azim'=32] {'axial'}, dimensions={0}, use_global_device_ids=true | all-gather | bytes 102400 | tf_op jit(solution)/shard_map/all_gather | solution.py:107
  179.5 1.7 broadcast_multiply_fusion
  181.4 16.4 %collective-permute-start.6 = (f32[5,64,3,128]{3,1,2,0:T(8,128)S(1)}, f32[5,64,3,128]{3,1,2,0:T(8,128)S(1)}, u32[]{:S(2)}, u32[]{:S(2)}) collective-permute-start(f32[5,64,3,128]{3,1,2,0:T(8,128)S(1)} %copy.26), channel_id=1, source_target_pairs={{1,0},{2,1},{3,2},{4,3},{5,4},{6,5},{7,6},{8,7},{9,8},{10,9},{11,1... | collective-permute-start | bytes 1474568 | tf_op jit(solution)/shard_map/ppermute | solution.py:28
  199.6 4.1 collective-permute-done.7
  204.0 1.7 fusion.36
  209.1 2.3 fusion.8
  211.5 56.8 %all-gather.9.cloned.1.call-done = f32[64,5,64,128]{3,2,1,0:T(8,128)} async-done(((f32[2,5,64,128]{3,2,1,0:T(8,128)}), f32[64,5,64,128]{3,2,1,0:T(8,128)}) %all-gather.9.cloned.1.call-update) | async-done | bytes 10485776 | tf_op jit(solution)/shard_map/all_gather | solution.py:145
  268.3 5.2 %slice_bitcast_fusion.1 = (f32[32,5,64,128]{3,2,1,0:T(8,128)S(1)}, f32[32,5,64,128]{3,2,1,0:T(8,128)S(1)}) fusion(f32[32,2,5,64,128]{4,3,2,1,0:T(8,128)} %bitcast.356), kind=kLoop, calls=%fused_computation.2 | loop fusion | bytes 20971520 | tf_op jit(solution)/shard_map/squeeze | solution.py:154
  273.5 5.4 %fusion.2 = f32[1,5,64,128]{3,0,2,1:T(1,128)S(1)} fusion(f32[32,5,64,128]{3,2,1,0:T(8,128)S(1)} %get-tuple-element.10, s32[]{:T(128)S(6)} %axis_index.33), kind=kOutput, calls=%fused_computation.7 | convolution fusion | flops 15729728 | bytes 5406724 | tf_op jit(solution)/shard_map/k,kvrx->vrx/dot_general | solution.py:154
  278.9 5.6 %fusion = f32[1,5,64,128]{3,0,2,1:T(1,128)S(1)} fusion(f32[32,5,64,128]{3,2,1,0:T(8,128)S(1)} %get-tuple-element.11, s32[]{:T(128)S(6)} %axis_index.33), kind=kOutput, calls=%fused_computation.5 | convolution fusion | flops 15729728 | bytes 5406724 | tf_op jit(solution)/shard_map/k,kvrx->vrx/dot_general | solution.py:155
  286.0 22.6 %scatter_custom_fusion = f32[65536]{0:T(1024)} fusion(s32[4096]{0:T(1024)S(1)} %add_bitcast_fusion, f32[4096]{0:T(1024)S(1)} %bitcast_multiply_fusion.21, f32[]{:T(128)} %constant.254.clone.1), kind=kCustom, calls=%fused_computation.160 | custom fusion | flops 4096 | bytes 262148 | tf_op jit(solution)/shard_map/scatter-add | solution.py:195
  308.6 140.8 %all-reduce.3.cloned.1.call-done = f32[512,128]{1,0:T(8,128)} async-done(((f32[512,128]{1,0:T(8,128)}), f32[512,128]{1,0:T(8,128)}) %all-reduce.3.cloned.1.call-update) | async-done | bytes 262160
  (124 shorter events, 34.4 us)
Async XLA Ops:
  7.2 201.9 %copy-start = (f32[256]{0:T(256)S(1)}, f32[256]{0:T(256)}, u32[]{:S(2)}) copy-start(f32[256]{0:T(256)} %param.23) | copy-start | bytes 3076
  7.2 2.8 copy-start.1
  7.2 2.8 copy-start.8
  7.2 2.8 copy-start.4
  7.2 2.8 copy-start.6
  7.2 90.1 %all-gather.7.cloned.1.call-start = ((), (), s32[]{:S(2)}) async-start(), calls=%async_computation | async-start | bytes 10813440 | tf_op jit(solution)/shard_map/all_gather | solution.py:145
  12.4 14.7 %copy-start.12 = (f32[64,8,128]{2,1,0:T(8,128)}, f32[64,8,128]{2,1,0:T(8,128)S(1)}, u32[]{:S(2)}) copy-start(f32[64,8,128]{2,1,0:T(8,128)S(1)} %get-tuple-element.3) | copy-start | bytes 786436
  12.7 9.3 %collective-permute-start.2 = (f32[5,64,3,128]{3,1,2,0:T(8,128)S(1)}, f32[5,64,3,128]{3,1,2,0:T(8,128)S(1)}, u32[]{:S(2)}, u32[]{:S(2)}) collective-permute-start(f32[5,64,3,128]{3,1,2,0:T(8,128)S(1)} %copy.18), channel_id=1, source_target_pairs={{1,0},{2,1},{3,2},{4,3},{5,4},{6,5},{7,6},{8,7},{9,8},{10,9},{11,1... | collective-permute-start | bytes 1474568 | tf_op jit(solution)/shard_map/ppermute | solution.py:28
  14.2 8.1 %collective-permute-start.3 = (f32[5,64,3,128]{3,1,2,0:T(8,128)S(1)}, f32[5,64,3,128]{3,1,2,0:T(8,128)S(1)}, u32[]{:S(2)}, u32[]{:S(2)}) collective-permute-start(f32[5,64,3,128]{3,1,2,0:T(8,128)S(1)} %copy.20), channel_id=1, source_target_pairs={{0,1},{1,2},{2,3},{3,4},{4,5},{5,6},{6,7},{7,8},{8,9},{9,10},{10,1... | collective-permute-start | bytes 1474568 | tf_op jit(solution)/shard_map/ppermute | solution.py:26
  23.8 2.5 copy-start.2
  25.0 2.1 copy-start.14
  27.1 241.2 %all-gather.9.cloned.1.call-start = ((), (), s32[]{:S(2)}) async-start(), calls=%async_computation.1 | async-start | bytes 10813440 | tf_op jit(solution)/shard_map/all_gather | solution.py:145
  30.4 9.1 %collective-permute-start = (f32[5,64,8,3]{1,2,3,0:T(8,128)S(1)}, f32[5,64,8,3]{1,2,3,0:T(8,128)S(1)}, u32[]{:S(2)}, u32[]{:S(2)}) collective-permute-start(f32[5,64,8,3]{1,2,3,0:T(8,128)S(1)} %copy.14), channel_id=1, source_target_pairs={{32,0},{64,32},{96,64},{33,1},{65,33},{97,65},{34,2},{66,34},{98,6... | collective-permute-start | bytes 92168 | tf_op jit(solution)/shard_map/ppermute | solution.py:28
  32.8 8.3 %collective-permute-start.1 = (f32[5,64,8,3]{1,2,3,0:T(8,128)}, f32[5,64,8,3]{1,2,3,0:T(8,128)S(1)}, u32[]{:S(2)}, u32[]{:S(2)}) collective-permute-start(f32[5,64,8,3]{1,2,3,0:T(8,128)} %copy.16), channel_id=1, source_target_pairs={{0,32},{32,64},{64,96},{1,33},{33,65},{65,97},{2,34},{34,66},{66,9... | collective-permute-start | bytes 92168 | tf_op jit(solution)/shard_map/ppermute | solution.py:26
  102.5 11.1 %copy-start.22 = (f32[5,64,8,128]{3,2,1,0:T(8,128)S(1)}, f32[5,64,8,128]{3,2,1,0:T(8,128)}, u32[]{:S(2)}) copy-start(f32[5,64,8,128]{3,2,1,0:T(8,128)} %fusion.19) | copy-start | bytes 3932164
  107.9 5.7 %copy-start.3 = (f32[5,64,8,128]{3,2,1,0:T(8,128)S(1)}, f32[5,64,8,128]{3,2,1,0:T(8,128)}, u32[]{:S(2)}) copy-start(f32[5,64,8,128]{3,2,1,0:T(8,128)} %copy-done.2) | copy-start | bytes 3932164
  107.9 5.7 %copy-start.5 = (f32[64,8,128]{2,1,0:T(8,128)S(1)}, f32[64,8,128]{2,1,0:T(8,128)}, u32[]{:S(2)}) copy-start(f32[64,8,128]{2,1,0:T(8,128)} %param.17) | copy-start | bytes 786436
  107.9 5.7 %copy-start.10 = (f32[64,8,128]{2,1,0:T(8,128)S(1)}, f32[64,8,128]{2,1,0:T(8,128)}, u32[]{:S(2)}) copy-start(f32[64,8,128]{2,1,0:T(8,128)} %param.12) | copy-start | bytes 786436
  107.9 5.7 %copy-start.13 = (f32[64,8,128]{2,1,0:T(8,128)S(1)}, f32[64,8,128]{2,1,0:T(8,128)}, u32[]{:S(2)}) copy-start(f32[64,8,128]{2,1,0:T(8,128)} %copy-done.12) | copy-start | bytes 786436
  107.9 5.7 %copy-start.15 = (f32[3,64,8,128]{3,2,1,0:T(8,128)S(1)}, f32[3,64,8,128]{3,2,1,0:T(8,128)}, u32[]{:S(2)}) copy-start(f32[3,64,8,128]{3,2,1,0:T(8,128)} %broadcast_multiply_fusion.1) | copy-start | bytes 2359300
  108.0 5.7 %copy-start.19 = (f32[5,64,8,128]{3,2,1,0:T(8,128)S(1)}, f32[5,64,8,128]{3,2,1,0:T(8,128)}, u32[]{:S(2)}) copy-start(f32[5,64,8,128]{3,2,1,0:T(8,128)} %param.18) | copy-start | bytes 3932164
  108.0 5.7 %copy-start.21 = (f32[8]{0:T(128)S(1)}, f32[8]{0:T(128)}, u32[]{:S(2)}) copy-start(f32[8]{0:T(128)} %get-tuple-element.39) | copy-start | bytes 100
  118.7 5.8 %collective-permute-start.4 = (f32[5,64,8,3]{1,2,3,0:T(8,128)S(1)}, f32[5,64,8,3]{1,2,3,0:T(8,128)S(1)}, u32[]{:S(2)}, u32[]{:S(2)}) collective-permute-start(f32[5,64,8,3]{1,2,3,0:T(8,128)S(1)} %copy.22), channel_id=1, source_target_pairs={{32,0},{64,32},{96,64},{33,1},{65,33},{97,65},{34,2},{66,34},{98,6... | collective-permute-start | bytes 92168 | tf_op jit(solution)/shard_map/ppermute | solution.py:28
  120.5 5.6 %collective-permute-start.5 = (f32[5,64,8,3]{1,2,3,0:T(8,128)S(1)}, f32[5,64,8,3]{1,2,3,0:T(8,128)S(1)}, u32[]{:S(2)}, u32[]{:S(2)}) collective-permute-start(f32[5,64,8,3]{1,2,3,0:T(8,128)S(1)} %copy.24), channel_id=1, source_target_pairs={{0,32},{32,64},{64,96},{1,33},{33,65},{65,97},{2,34},{34,66},{66,9... | collective-permute-start | bytes 92168 | tf_op jit(solution)/shard_map/ppermute | solution.py:26
  181.4 17.9 %collective-permute-start.6 = (f32[5,64,3,128]{3,1,2,0:T(8,128)S(1)}, f32[5,64,3,128]{3,1,2,0:T(8,128)S(1)}, u32[]{:S(2)}, u32[]{:S(2)}) collective-permute-start(f32[5,64,3,128]{3,1,2,0:T(8,128)S(1)} %copy.26), channel_id=1, source_target_pairs={{1,0},{2,1},{3,2},{4,3},{5,4},{6,5},{7,6},{8,7},{9,8},{10,9},{11,1... | collective-permute-start | bytes 1474568 | tf_op jit(solution)/shard_map/ppermute | solution.py:28
  197.8 5.8 %collective-permute-start.7 = (f32[5,64,3,128]{3,1,2,0:T(8,128)S(1)}, f32[5,64,3,128]{3,1,2,0:T(8,128)S(1)}, u32[]{:S(2)}, u32[]{:S(2)}) collective-permute-start(f32[5,64,3,128]{3,1,2,0:T(8,128)S(1)} %copy.28), channel_id=1, source_target_pairs={{0,1},{1,2},{2,3},{3,4},{4,5},{5,6},{6,7},{7,8},{8,9},{9,10},{10,1... | collective-permute-start | bytes 1474568 | tf_op jit(solution)/shard_map/ppermute | solution.py:26
  207.0 2.1 copy-start.20
  208.2 3.2 copy-start.16
  208.2 3.2 copy-start.17
  209.0 240.4 %all-reduce.3.cloned.1.call-start = ((), (), s32[]{:S(2)}) async-start(), calls=%async_computation.2 | async-start | bytes 524288
  284.5 1.5 copy-start.18
  286.0 164.7 %copy-start.11 = (f32[5,64,8,128]{3,2,1,0:T(8,128)}, f32[5,64,8,128]{3,2,1,0:T(8,128)S(1)}, u32[]{:S(2)}) copy-start(f32[5,64,8,128]{3,2,1,0:T(8,128)S(1)} %fusion.17) | copy-start | bytes 3932164
  (2 other events, 2.1 us)
Sparse Core Ops, SparseCore 0:
  27.2 63.5 all-gather.6
  209.2 59.0 all-gather.8
  308.8 140.6 all-reduce.2
where the time goes:
time: 464 us; the launch traced here: 457 us
  waiting for transfers between devices  209 us (45%)
  matrix products  108 us (23%)
  other arithmetic  44.7 us (10%)
  local copies, waits for them, and re-layouts  30.9 us (7%)
  starting transfers between devices  30.1 us (6%)
  blocking collectives  19.1 us (4%)
  between operations  14.7 us (3%)
    unnamed x4, waiting for transfers between devices  141 us
    all_gather x2, waiting for transfers between devices, cycle_line(): piece = lax.all_gather(moments, 'azim', axis=0, tiled=True)  56.8 us
    dot_general x2, matrix products, open_line(): jnp.einsum('vraj,j->vra', rhs, signed_power(base, offsets), precision=HIG...  35.4 us
    dot_general x2, matrix products, open_line(): jnp.einsum('vraj,j->vra', rhs, signed_power(base, width_here - 1 - offset...  34.6 us
    scatter-add x1, other arithmetic, per_device(): jax.ops.segment_sum(values, bucket, num_segments=OBSERVERS * TIME_BINS)  22.6 us
    ppermute x4, starting transfers between devices, padded(): lax.ppermute(head, axis, [((i + 1) % count, i) for i in range(ends)])  20.4 us
    all_gather x2, blocking collectives, open_line(): piece = lax.all_gather(moments, 'axial', axis=0, tiled=True)  19.1 us
    dot_general x2, matrix products, cycle_line(): last_sum = jnp.einsum('k,kvrx->vrx', w_last, piece[:, 1], precision=HIGHEST)  11.2 us
  transfers between devices with their start and end apart: 11, of which 5 were waited for; matrix products, arithmetic and copies ran while one was open for 13% of the time, Pallas kernels for 0%

commit v1 on v0

--- a/solution.py
+++ b/solution.py
@@ -142,7 +142,11 @@
     )
     last_moment = jnp.einsum("vrjx,j->vrx", rhs, signed_power(base, offsets), precision=HIGHEST)
     moments = jnp.stack([first_moment, last_moment])[None]
-    piece = lax.all_gather(moments, "azim", axis=0, tiled=True)
+    devices = lax.axis_size("azim")
+    repeats = [devices if d == 0 else 1 for d in range(moments.ndim)]
+    piece = lax.all_to_all(
+        jnp.tile(moments, repeats), "azim", split_axis=0, concat_axis=0, tiled=True
+    )
     others = jnp.arange(piece.shape[0], dtype=jnp.int32)
     shift = (device_pos - others) % group_size
     w_first = jnp.where(

time: 464 us -> 620 us (1.34)
  waiting for transfers between devices: 209 us -> 334 us
  starting transfers between devices: 30.1 us -> 50.7 us
  local copies, waits for them, and re-layouts: 30.9 us -> 41.3 us
    all_to_all x0 -> x2, waiting for transfers between devices: none -> 177 us  [cycle_line(): lax.all_to_all(jnp.tile(moments, repeats), 'azim', split_axis=0, concat_a...]
    all_gather x2 -> x0, waiting for transfers between devices: 56.8 us -> none  [cycle_line(): piece = lax.all_gather(moments, 'azim', axis=0, tiled=True)]
    all_to_all x0 -> x2, starting transfers between devices: none -> 24.7 us  [cycle_line(): lax.all_to_all(jnp.tile(moments, repeats), 'azim', split_axis=0, concat_a...]
    another operation x0 -> x2, local copies, waits for them, and re-layouts: none -> 10.4 us  [cycle_line(): jnp.tile(moments, repeats)]
    unnamed x4 -> x2, waiting for transfers between devices: 141 us -> 145 us
  transfers between devices with their start and end apart: 11 -> 11, of which waited for: 5 -> 6; matrix products, arithmetic and copies ran while one was open for 13% -> 10% of each run, Pallas kernels for 0% -> 0%
where the time goes in v1:
time: 620 us; the launch traced here: 613 us
  waiting for transfers between devices  334 us (54%)
  matrix products  108 us (17%)
  starting transfers between devices  50.7 us (8%)
  other arithmetic  42.6 us (7%)
  local copies, waits for them, and re-layouts  41.3 us (7%)
  blocking collectives  20.5 us (3%)
  between operations  15 us (2%)
    all_to_all x2, waiting for transfers between devices, cycle_line(): lax.all_to_all(jnp.tile(moments, repeats), 'azim', split_axis=0, concat_a...  177 us
    unnamed x2, waiting for transfers between devices  145 us
    dot_general x2, matrix products, open_line(): jnp.einsum('vraj,j->vra', rhs, signed_power(base, offsets), precision=HIG...  35.4 us
    dot_general x2, matrix products, open_line(): jnp.einsum('vraj,j->vra', rhs, signed_power(base, width_here - 1 - offset...  34.6 us
    all_to_all x2, starting transfers between devices, cycle_line(): lax.all_to_all(jnp.tile(moments, repeats), 'azim', split_axis=0, concat_a...  24.7 us
    scatter-add x1, other arithmetic, per_device(): jax.ops.segment_sum(values, bucket, num_segments=OBSERVERS * TIME_BINS)  22.6 us
    all_gather x2, blocking collectives, open_line(): piece = lax.all_gather(moments, 'axial', axis=0, tiled=True)  20.5 us
    ppermute x4, starting transfers between devices, padded(): lax.ppermute(head, axis, [((i + 1) % count, i) for i in range(ends)])  16.4 us
  transfers between devices with their start and end apart: 11, of which 6 were waited for; matrix products, arithmetic and copies ran while one was open for 10% of the time, Pallas kernels for 0%

profile of v1, /device:TPU:1, one launch (start us, length us, event | category | flops | bytes accessed | tf_op | source)
XLA Modules:
  0.0 612.8 jit_solution(8884503430977676030)
XLA Ops:
  7.2 2.0 bitcast_dynamic-update-slice_fusion.4
  14.9 6.4 %collective-permute-done.2 = f32[5,64,3,128]{3,1,2,0:T(8,128)S(1)} collective-permute-done((f32[5,64,3,128]{3,1,2,0:T(8,128)S(1)}, f32[5,64,3,128]{3,1,2,0:T(8,128)S(1)}, u32[]{:S(2)}, u32[]{:S(2)}) %collective-permute-start.2) | collective-permute-done | bytes 491552 | tf_op jit(solution)/shard_map/ppermute | solution.py:28
  25.6 5.2 tile.4
  30.8 14.2 %all-to-all-start = ((f32[32,2,5,64,128]{4,3,2,1,0:T(8,128)}), f32[32,2,5,64,128]{4,3,2,1,0:T(8,128)}, u32[]{:S(2)}, u32[]{:S(2)}) async-start(f32[32,2,5,64,128]{4,3,2,1,0:T(8,128)} %tile.4), calls=%async_computation | async-start | bytes 20971520 | tf_op jit(solution)/shard_map/all_to_all | solution.py:147
  50.7 4.2 collective-permute-start.1
  55.4 1.9 broadcast_multiply_fusion.1
  60.5 5.6 fusion.30
  66.1 17.3 %fusion.215 = f32[1,5,64,8]{3,0,2,1:T(1,128)S(1)} fusion(f32[5,64,8,128]{3,2,1,0:T(8,128)S(1)} %fusion.30), kind=kOutput, calls=%fused_computation.350 | convolution fusion | flops 3934336 | bytes 1320960 | tf_op jit(solution)/shard_map/vraj,j->vra/dot_general | solution.py:102
  83.6 17.7 %fusion.213 = f32[1,5,64,8]{3,0,2,1:T(1,128)S(1)} fusion(f32[5,64,8,128]{3,2,1,0:T(8,128)S(1)} %fusion.30), kind=kOutput, calls=%fused_computation.348 | convolution fusion | flops 3933568 | bytes 1320960 | tf_op jit(solution)/shard_map/vraj,j->vra/dot_general | solution.py:105
  101.4 10.7 %all-gather = f32[8,5,64,8]{2,3,1,0:T(8,128)S(1)} all-gather(f32[2,5,64,8]{2,3,1,0:T(8,128)S(1)} %pad_maximum_fusion.10), channel_id=2, replica_groups=mesh['axial'=4,'azim'=32] {'axial'}, dimensions={0}, use_global_device_ids=true | all-gather | bytes 102400 | tf_op jit(solution)/shard_map/all_gather | solution.py:107
  113.4 2.5 fusion.19
  115.9 54.4 %all-to-all-done = f32[32,2,5,64,128]{4,3,2,1,0:T(8,128)} async-done(((f32[32,2,5,64,128]{4,3,2,1,0:T(8,128)}), f32[32,2,5,64,128]{4,3,2,1,0:T(8,128)}, u32[]{:S(2)}, u32[]{:S(2)}) %all-to-all-start) | async-done | bytes 10485792 | tf_op jit(solution)/shard_map/all_to_all | solution.py:147
  170.3 5.2 slice_bitcast_fusion.3
  175.5 5.4 fusion.6
  181.0 5.6 fusion.4
  186.6 1.8 fusion.21
  193.5 4.0 collective-permute-start.5
  200.6 6.2 %fusion.47 = f32[5,64,8,128]{3,2,1,0:T(8,128)S(1)} fusion(f32[5,64,8,3]{3,2,1,0:T(8,128)} %copy.25, f32[5,64,8,128]{3,2,1,0:T(8,128)S(1)} %fusion.21, f32[5,64,8,3]{3,2,1,0:T(8,128)} %copy.23), kind=kLoop, calls=%fused_computation.81 | loop fusion | flops 5242880 | bytes 2682880 | tf_op jit(solution)/shard_map/add | solution.py:69
  206.9 17.3 %fusion.204 = f32[1,5,64,8]{3,0,2,1:T(1,128)S(1)} fusion(f32[5,64,8,128]{3,2,1,0:T(8,128)S(1)} %fusion.47), kind=kOutput, calls=%fused_computation.339 | convolution fusion | flops 3934336 | bytes 1320960 | tf_op jit(solution)/shard_map/vraj,j->vra/dot_general | solution.py:102
  224.1 17.7 %fusion.202 = f32[1,5,64,8]{3,0,2,1:T(1,128)S(1)} fusion(f32[5,64,8,128]{3,2,1,0:T(8,128)S(1)} %fusion.47), kind=kOutput, calls=%fused_computation.337 | convolution fusion | flops 3933568 | bytes 1320960 | tf_op jit(solution)/shard_map/vraj,j->vra/dot_general | solution.py:105
  242.1 9.7 %all-gather.1 = f32[8,5,64,8]{2,3,1,0:T(8,128)S(1)} all-gather(f32[2,5,64,8]{2,3,1,0:T(8,128)S(1)} %pad_maximum_fusion.11), channel_id=3, replica_groups=mesh['axial'=4,'azim'=32] {'axial'}, dimensions={0}, use_global_device_ids=true | all-gather | bytes 102400 | tf_op jit(solution)/shard_map/all_gather | solution.py:107
  255.0 12.3 %collective-permute-start.6 = (f32[5,64,3,128]{3,1,2,0:T(8,128)S(1)}, f32[5,64,3,128]{3,1,2,0:T(8,128)S(1)}, u32[]{:S(2)}, u32[]{:S(2)}) collective-permute-start(f32[5,64,3,128]{3,1,2,0:T(8,128)S(1)} %copy.26), channel_id=1, source_target_pairs={{1,0},{2,1},{3,2},{4,3},{5,4},{6,5},{7,6},{8,7},{9,8},{10,9},{11,1... | collective-permute-start | bytes 1474568 | tf_op jit(solution)/shard_map/ppermute | solution.py:28
  269.2 4.1 collective-permute-done.7
  277.8 5.2 tile.5
  283.0 10.5 %all-to-all-start.1 = ((f32[32,2,5,64,128]{4,3,2,1,0:T(8,128)}), f32[32,2,5,64,128]{4,3,2,1,0:T(8,128)}, u32[]{:S(2)}, u32[]{:S(2)}) async-start(f32[32,2,5,64,128]{4,3,2,1,0:T(8,128)} %tile.5), calls=%async_computation.1 | async-start | bytes 20971520 | tf_op jit(solution)/shard_map/all_to_all | solution.py:147
  293.6 2.3 fusion.8
  295.9 122.8 %all-to-all-done.1 = f32[32,2,5,64,128]{4,3,2,1,0:T(8,128)} async-done(((f32[32,2,5,64,128]{4,3,2,1,0:T(8,128)}), f32[32,2,5,64,128]{4,3,2,1,0:T(8,128)}, u32[]{:S(2)}, u32[]{:S(2)}) %all-to-all-start.1) | async-done | bytes 10485792 | tf_op jit(solution)/shard_map/all_to_all | solution.py:147
  418.8 5.2 slice_bitcast_fusion.1
  424.0 5.4 fusion.2
  429.4 5.6 fusion
  436.5 22.6 %scatter_custom_fusion = f32[65536]{0:T(1024)} fusion(s32[4096]{0:T(1024)S(1)} %add_bitcast_fusion, f32[4096]{0:T(1024)S(1)} %bitcast_multiply_fusion.21, f32[]{:T(128)} %constant.254.clone.1), kind=kCustom, calls=%fused_computation.160 | custom fusion | flops 4096 | bytes 262148 | tf_op jit(solution)/shard_map/scatter-add | solution.py:199
  459.1 145.3 %all-reduce.3.cloned.1.call-done = f32[512,128]{1,0:T(8,128)} async-done(((f32[512,128]{1,0:T(8,128)}), f32[512,128]{1,0:T(8,128)}) %all-reduce.3.cloned.1.call-update) | async-done | bytes 262160
  (122 shorter events, 41.4 us)
Async XLA Ops:
  7.2 286.4 %copy-start = (f32[256]{0:T(256)S(1)}, f32[256]{0:T(256)}, u32[]{:S(2)}) copy-start(f32[256]{0:T(256)} %param.23) | copy-start | bytes 3076
  7.2 2.1 copy-start.1
  7.2 2.2 copy-start.8
  7.2 2.3 copy-start.4
  7.2 2.3 copy-start.6
  9.3 1.2 copy-start.7
  11.8 33.2 %copy-start.12 = (f32[64,8,128]{2,1,0:T(8,128)}, f32[64,8,128]{2,1,0:T(8,128)S(1)}, u32[]{:S(2)}) copy-start(f32[64,8,128]{2,1,0:T(8,128)S(1)} %get-tuple-element.3) | copy-start | bytes 786436
  12.0 9.3 %collective-permute-start.2 = (f32[5,64,3,128]{3,1,2,0:T(8,128)S(1)}, f32[5,64,3,128]{3,1,2,0:T(8,128)S(1)}, u32[]{:S(2)}, u32[]{:S(2)}) collective-permute-start(f32[5,64,3,128]{3,1,2,0:T(8,128)S(1)} %copy.18), channel_id=1, source_target_pairs={{1,0},{2,1},{3,2},{4,3},{5,4},{6,5},{7,6},{8,7},{9,8},{10,9},{11,1... | collective-permute-start | bytes 1474568 | tf_op jit(solution)/shard_map/ppermute | solution.py:28
  13.6 8.1 %collective-permute-start.3 = (f32[5,64,3,128]{3,1,2,0:T(8,128)S(1)}, f32[5,64,3,128]{3,1,2,0:T(8,128)S(1)}, u32[]{:S(2)}, u32[]{:S(2)}) collective-permute-start(f32[5,64,3,128]{3,1,2,0:T(8,128)S(1)} %copy.20), channel_id=1, source_target_pairs={{0,1},{1,2},{2,3},{3,4},{4,5},{5,6},{6,7},{7,8},{8,9},{9,10},{10,1... | collective-permute-start | bytes 1474568 | tf_op jit(solution)/shard_map/ppermute | solution.py:26
  23.2 2.4 copy-start.2
  30.8 139.4 %all-to-all-start = ((f32[32,2,5,64,128]{4,3,2,1,0:T(8,128)}), f32[32,2,5,64,128]{4,3,2,1,0:T(8,128)}, u32[]{:S(2)}, u32[]{:S(2)}) async-start(f32[32,2,5,64,128]{4,3,2,1,0:T(8,128)} %tile.4), calls=%async_computation | async-start | bytes 20971520 | tf_op jit(solution)/shard_map/all_to_all | solution.py:147
  48.3 9.1 %collective-permute-start = (f32[5,64,8,3]{1,2,3,0:T(8,128)S(1)}, f32[5,64,8,3]{1,2,3,0:T(8,128)S(1)}, u32[]{:S(2)}, u32[]{:S(2)}) collective-permute-start(f32[5,64,8,3]{1,2,3,0:T(8,128)S(1)} %copy.14), channel_id=1, source_target_pairs={{32,0},{64,32},{96,64},{33,1},{65,33},{97,65},{34,2},{66,34},{98,6... | collective-permute-start | bytes 92168 | tf_op jit(solution)/shard_map/ppermute | solution.py:28
  50.7 8.3 %collective-permute-start.1 = (f32[5,64,8,3]{1,2,3,0:T(8,128)}, f32[5,64,8,3]{1,2,3,0:T(8,128)S(1)}, u32[]{:S(2)}, u32[]{:S(2)}) collective-permute-start(f32[5,64,8,3]{1,2,3,0:T(8,128)} %copy.16), channel_id=1, source_target_pairs={{0,32},{32,64},{64,96},{1,33},{33,65},{65,97},{2,34},{34,66},{66,9... | collective-permute-start | bytes 92168 | tf_op jit(solution)/shard_map/ppermute | solution.py:26
  175.4 11.1 %copy-start.21 = (f32[5,64,8,128]{3,2,1,0:T(8,128)S(1)}, f32[5,64,8,128]{3,2,1,0:T(8,128)}, u32[]{:S(2)}) copy-start(f32[5,64,8,128]{3,2,1,0:T(8,128)} %fusion.19) | copy-start | bytes 3932164
  180.9 5.7 copy-start.3
  180.9 5.7 copy-start.5
  180.9 5.7 copy-start.10
  180.9 5.7 copy-start.13
  180.9 5.7 copy-start.14
  180.9 5.7 copy-start.18
  180.9 5.7 copy-start.20
  191.7 5.8 collective-permute-start.4
  193.5 5.6 collective-permute-start.5
  255.0 13.8 %collective-permute-start.6 = (f32[5,64,3,128]{3,1,2,0:T(8,128)S(1)}, f32[5,64,3,128]{3,1,2,0:T(8,128)S(1)}, u32[]{:S(2)}, u32[]{:S(2)}) collective-permute-start(f32[5,64,3,128]{3,1,2,0:T(8,128)S(1)} %copy.26), channel_id=1, source_target_pairs={{1,0},{2,1},{3,2},{4,3},{5,4},{6,5},{7,6},{8,7},{9,8},{10,9},{11,1... | collective-permute-start | bytes 1474568 | tf_op jit(solution)/shard_map/ppermute | solution.py:28
  267.4 5.8 collective-permute-start.7
  283.0 10.6 %copy-start.19 = (s32[4,8,128]{2,1,0:T(8,128)S(1)}, s32[4,8,128]{2,1,0:T(8,128)}, u32[]{:S(2)}) copy-start(s32[4,8,128]{2,1,0:T(8,128)} %param.22) | copy-start | bytes 49156
  283.0 12.9 %copy-start.15 = (s32[4,8,128]{2,1,0:T(8,128)S(1)}, s32[4,8,128]{2,1,0:T(8,128)}, u32[]{:S(2)}) copy-start(s32[4,8,128]{2,1,0:T(8,128)} %param.21) | copy-start | bytes 49156
  283.0 12.9 %copy-start.16 = (s32[4,8,128]{2,1,0:T(8,128)S(1)}, s32[4,8,128]{2,1,0:T(8,128)}, u32[]{:S(2)}) copy-start(s32[4,8,128]{2,1,0:T(8,128)} %param.20) | copy-start | bytes 49156
  283.0 135.8 %all-to-all-start.1 = ((f32[32,2,5,64,128]{4,3,2,1,0:T(8,128)}), f32[32,2,5,64,128]{4,3,2,1,0:T(8,128)}, u32[]{:S(2)}, u32[]{:S(2)}) async-start(f32[32,2,5,64,128]{4,3,2,1,0:T(8,128)} %tile.5), calls=%async_computation.1 | async-start | bytes 20971520 | tf_op jit(solution)/shard_map/all_to_all | solution.py:147
  293.5 310.9 %all-reduce.3.cloned.1.call-start = ((), (), s32[]{:S(2)}) async-start(), calls=%async_computation.2 | async-start | bytes 524288
  435.0 1.5 copy-start.17
  436.5 169.2 %copy-start.11 = (f32[5,64,8,128]{3,2,1,0:T(8,128)}, f32[5,64,8,128]{3,2,1,0:T(8,128)S(1)}, u32[]{:S(2)}) copy-start(f32[5,64,8,128]{3,2,1,0:T(8,128)S(1)} %fusion.17) | copy-start | bytes 3932164
  (1 other events, 1.0 us)
Sparse Core Ops, SparseCore 0:
  459.3 145.1 all-reduce.2
